TPU v7x, 512 devices: a whole 4x4x16 slice. The times are simulated.
512 devices in a mesh: seg: 8 (over x, core), blk: 64 (over y, z).
Axes of the slice: x: 4, y: 4, z: 16, core: 2. Of those that a mesh axis runs over, the one named last changes fastest.
Arguments:
- products: bfloat16 [8, 4096, 16384], P('seg', 'blk'), may hold values from -0.09375 to 0.09375
- compat: int32 [8, 64, 16], P('seg', 'blk'), may hold values 0 or 1
- sizes: int32 [8, 64], P('seg', 'blk'), may hold values from 1 to 256, 12288 in all within a row
Outputs:
- orthonormal: bfloat16 [8, 4096, 16384], P('seg', None, 'blk')
- accumulated: float32 [8, 64, 256, 256], P('seg', 'blk')
Inputs may be any that keep to these rules, and one draw needn't show every extreme that they name: Each site's 64 sector sizes sum to 12288 and one of them is exactly 256.
All inputs are finite; a program needn't handle non-finite values. No bound on the sum of `compat` or of `sizes` on one device may be relied on, other than what follows from the above.
Results may differ from a plain program's by a relative error of at most 0.001.
Values may be sent and summed in bfloat16 or wider, within the bound.
A program may use at most 64 MiB of HBM per device.

v0:
```python
import jax
import jax.numpy as jnp
from jax import lax
from jax.sharding import PartitionSpec as P

B = 256


shift_value = 0.05


def split_up(x, dim, length):
    dims = x.shape
    parts = x.reshape(*dims[:dim], length, dims[dim] // length, *dims[dim + 1 :])
    return jnp.moveaxis(parts, dim, 0)


def edges_of(length, count):
    hop = length // count
    if hop >= 8:
        hop -= hop % 8
    return [hop * k for k in range(1, count)]


def laid_out(parts, dim):
    parts = jnp.moveaxis(parts, 0, dim)
    dims = parts.shape
    return parts.reshape(*dims[:dim], dims[dim] * dims[dim + 1], *dims[dim + 2 :])


def several_exchanges(x, axis, pieces, split_dim, concat_dim):
    parts = split_up(x, split_dim, lax.axis_size(axis))
    cut = max(range(1, max(2, parts.ndim - 1)), key=lambda d: parts.shape[d])
    done = []
    for share in jnp.split(parts, edges_of(parts.shape[cut], pieces), axis=cut):
        if share.size:
            done.append(lax.all_to_all(share, axis, split_axis=0, concat_axis=0, tiled=True))
    return laid_out(jnp.concatenate(done, axis=cut), concat_dim)


def entering(part, axis, combine, identity):
    place = lax.axis_index(axis)
    gathered = jax.tree.map(lambda a: lax.all_gather(a, axis), part)
    state = jax.tree.map(lambda a, e: jnp.zeros_like(a) + jnp.asarray(e, a.dtype), part, identity)

    def one(hop, state):
        return combine(
            state, jax.tree.map(lambda a: lax.dynamic_index_in_dim(a, hop, 0, False), gathered)
        )

    return lax.fori_loop(0, place, one, state)


def factor_sector(panel_in, allowed, live_cols):
    total_rows = panel_in.shape[0]
    width_cols = panel_in.shape[1]
    gate_rows = jnp.repeat(
        allowed, total_rows // allowed.shape[0], total_repeat_length=total_rows
    ).astype(jnp.bfloat16)
    masked = panel_in * gate_rows[:, None] * live_cols.astype(jnp.bfloat16)[None, :]
    gram_raw = jnp.dot(masked.T, masked, preferred_element_type=jnp.float32)
    identity = jnp.eye(width_cols, dtype=jnp.float32)
    lower_one = jnp.linalg.cholesky(gram_raw + shift_value * identity)
    first_t = jax.scipy.linalg.solve_triangular(lower_one, masked.astype(jnp.float32).T, lower=True)
    gram_two = jnp.dot(first_t, first_t.T, precision=lax.Precision.HIGHEST) + shift_value * identity
    lower_two = jnp.linalg.cholesky(gram_two)
    ortho_t = jax.scipy.linalg.solve_triangular(lower_two, first_t, lower=True)
    factor_r = jnp.dot(lower_two.T, lower_one.T, precision=lax.Precision.HIGHEST)
    return (ortho_t.T.astype(jnp.bfloat16), factor_r)


def compose(earlier, later):
    return jnp.einsum("kab,kbc->kac", later, earlier, precision=lax.Precision.HIGHEST)


def local(products, compat, sizes):
    relayed = several_exchanges(products, "blk", 2, 2, 1)
    sectors_here = sizes.shape[1]
    total_rows = relayed.shape[1]
    panels = relayed[0].reshape(total_rows, sectors_here, B).transpose(1, 0, 2)
    live = (jnp.arange(B, dtype=jnp.int32)[None, :] < sizes[0][:, None]).astype(jnp.int32)
    ortho, factors = jax.vmap(factor_sector)(panels, compat[0], live)
    ortho_out = ortho.transpose(1, 0, 2).reshape(1, total_rows, sectors_here * B)
    identity = jnp.broadcast_to(jnp.eye(B, dtype=jnp.float32), (sectors_here, B, B))
    before = entering(factors, "seg", compose, identity)
    accumulated = compose(before, factors)
    return (ortho_out, accumulated[None])


def solution(mesh):
    in_specs = (P("seg", "blk", None), P("seg", "blk", None), P("seg", "blk"))
    out_specs = (P("seg", None, "blk"), P("seg", "blk", None, None))
    return jax.shard_map(local, mesh=mesh, in_specs=in_specs, out_specs=out_specs, check_vma=False)
```

profile of v0, /device:TPU:6, one launch (start us, length us, event | category | flops | bytes accessed | tf_op | source)
XLA Modules:
  0.0 307.9 jit_solution(5994773757957568905)
XLA Ops:
  7.2 2.1 copy.57
  11.3 18.7 %all-to-all-start = ((bf16[64,1,32,256]{3,2,1,0:T(8,128)(2,1)}), bf16[64,1,32,256]{3,2,1,0:T(8,128)(2,1)S(1)}, u32[]{:S(2)}, u32[]{:S(2)}) async-start(bf16[64,1,32,256]{3,2,1,0:T(8,128)(2,1)} %copy.39), calls=%async_computation | async-start | bytes 2097152 | tf_op jit(solution)/shard_map/all_to_all | solution.py:37
  31.8 52.1 %all-to-all-done = bf16[64,1,32,256]{3,2,1,0:T(8,128)(2,1)S(1)} async-done(((bf16[64,1,32,256]{3,2,1,0:T(8,128)(2,1)}), bf16[64,1,32,256]{3,2,1,0:T(8,128)(2,1)S(1)}, u32[]{:S(2)}, u32[]{:S(2)}) %all-to-all-start) | async-done | bytes 1048608 | tf_op jit(solution)/shard_map/all_to_all | solution.py:37
  83.9 6.7 %all-to-all-start.1 = ((bf16[64,1,32,256]{3,2,1,0:T(8,128)(2,1)}), bf16[64,1,32,256]{3,2,1,0:T(8,128)(2,1)S(1)}, u32[]{:S(2)}, u32[]{:S(2)}) async-start(bf16[64,1,32,256]{3,2,1,0:T(8,128)(2,1)} %copy.40), calls=%async_computation.1 | async-start | bytes 2097152 | tf_op jit(solution)/shard_map/all_to_all | solution.py:37
  91.8 10.2 %select_select_fusion = s32[4096]{0:T(1024)S(1)} fusion(pred[4096]{0:T(1024)(128)(4,1)S(1)} %copy-done.5, pred[4096]{0:T(1024)(128)(4,1)S(1)} %copy-done.6, pred[4096]{0:T(1024)(128)(4,1)S(1)} %copy-done.7, pred[4096]{0:T(1024)(128)(4,1)S(1)} %copy-done.8, pred[4096]{0:T(1024)(128)(4,1)S(1)} %copy-done.9, pred[4096]{0:T(1024)(128)(4,1)S(1)} %copy-done.10, ...), kind=kLoop, calls=%fused_computation.95 | loop fusion | flops 61440 | bytes 77888 | tf_op jit(solution)/shard_map/vmap(jit(_take))/gather | solution.py:57
  103.0 10.2 %fusion.63 = bf16[4096]{0:T(1024)(128)(2,1)S(1)} fusion(pred[4096]{0:T(1024)(128)(4,1)S(1)} %copy-done.5, pred[4096]{0:T(1024)(128)(4,1)S(1)} %copy-done.6, pred[4096]{0:T(1024)(128)(4,1)S(1)} %copy-done.7, pred[4096]{0:T(1024)(128)(4,1)S(1)} %copy-done.8, pred[4096]{0:T(1024)(128)(4,1)S(1)} %copy-done.9, pred[4096]{0:T(1024)(128)(4,1)S(1)} %copy-done.10, ...), kind=kLoop, calls=%fused_computation.109 | loop fusion | flops 65536 | bytes 69696 | tf_op jit(solution)/shard_map/vmap()/convert_element_type | solution.py:59
  113.3 31.1 %all-to-all-done.1 = bf16[64,1,32,256]{3,2,1,0:T(8,128)(2,1)S(1)} async-done(((bf16[64,1,32,256]{3,2,1,0:T(8,128)(2,1)}), bf16[64,1,32,256]{3,2,1,0:T(8,128)(2,1)S(1)}, u32[]{:S(2)}, u32[]{:S(2)}) %all-to-all-start.1) | async-done | bytes 1048608 | tf_op jit(solution)/shard_map/all_to_all | solution.py:37
  144.4 2.1 fusion.21
  146.7 11.7 %custom-call.17 = f32[1,128,128]{2,1,0:T(8,128)S(1)} custom-call(f32[1,128,128]{2,1,0:T(8,128)S(1)} %cholesky.191), custom_call_target="Cholesky" | custom-call | tf_op jit(solution)/shard_map/vmap(jit(cholesky))/cholesky | solution.py:63
  158.4 9.8 %custom-call.18 = f32[1,1,128,128]{2,3,1,0:T(8,128)S(1)} custom-call(f32[1,1,128,128]{3,2,1,0:T(8,128)S(1)} %get-tuple-element.123), custom_call_target="InvertDiagBlocksLowerTriangular" | custom-call | tf_op jit(solution)/shard_map/vmap(jit(cholesky))/cholesky | solution.py:63
  168.7 12.2 %custom-call.19 = f32[1,128,128]{2,1,0:T(8,128)S(1)} custom-call(f32[1,128,128]{2,1,0:T(8,128)S(1)} %fusion.24), custom_call_target="Cholesky" | custom-call | tf_op jit(solution)/shard_map/vmap(jit(cholesky))/cholesky | solution.py:63
  183.0 4.0 %while.16 = (s32[]{:T(128)}, f32[1,256,256]{2,1,0:T(8,128)S(1)}, s32[2,2]{1,0:T(2,128)S(1)}, f32[2,1,128,128]{3,2,1,0:T(8,128)S(1)}, s32[]{:T(128)}) while((s32[]{:T(128)}, f32[1,256,256]{2,1,0:T(8,128)S(1)}, s32[2,2]{1,0:T(2,128)S(1)}, f32[2,1,128,128]{3,2,1,0:T(8,128)S(1)}, s32[]{:T(128)}) %tuple.90), condition=%wide.while_cond.1, body=%wide.while_body.1.sunk | while | flops 2 | bytes 131181 | solution.py:64
  187.0 19.7 %custom-call.20 = f32[1,2,128,128]{2,3,1,0:T(8,128)S(1)} custom-call(f32[1,2,128,128]{3,2,1,0:T(8,128)S(1)} %bitcast.208), custom_call_target="InvertDiagBlocksLowerTriangular" | custom-call | tf_op jit(solution)/shard_map/vmap(jit(_solve_triangular))/triangular_solve | solution.py:64
  208.2 2.9 copy.47
  215.4 1.9 convolution_bitcast_fusion.3
  217.3 3.5 %fusion.28 = f32[256,256]{0,1:T(8,128)S(1)} fusion(f32[1,128,4096]{2,1,0:T(8,128)S(1)} %convolution_bitcast_fusion.3, f32[1,128,4096]{2,1,0:T(8,128)S(1)} %bitcast.195), kind=kOutput, calls=%fused_computation.42 | convolution fusion | flops 3222470656 | bytes 4456448 | tf_op jit(solution)/shard_map/vmap()/dot_general | solution.py:65
  221.1 11.9 %custom-call.21 = f32[1,128,128]{2,1,0:T(8,128)S(1)} custom-call(f32[1,128,128]{2,1,0:T(8,128)S(1)} %cholesky.194), custom_call_target="Cholesky" | custom-call | tf_op jit(solution)/shard_map/vmap(jit(cholesky))/cholesky | solution.py:66
  233.0 9.8 %custom-call.22 = f32[1,1,128,128]{2,3,1,0:T(8,128)S(1)} custom-call(f32[1,1,128,128]{3,2,1,0:T(8,128)S(1)} %get-tuple-element.119), custom_call_target="InvertDiagBlocksLowerTriangular" | custom-call | tf_op jit(solution)/shard_map/vmap(jit(cholesky))/cholesky | solution.py:66
  243.3 11.7 %custom-call.23 = f32[1,128,128]{2,1,0:T(8,128)S(1)} custom-call(f32[1,128,128]{2,1,0:T(8,128)S(1)} %fusion.25), custom_call_target="Cholesky" | custom-call | tf_op jit(solution)/shard_map/vmap(jit(cholesky))/cholesky | solution.py:66
  259.0 3.8 %while.17 = (s32[]{:T(128)}, f32[1,256,256]{2,1,0:T(8,128)S(1)}, s32[2,2]{1,0:T(2,128)S(1)}, f32[2,1,128,128]{3,2,1,0:T(8,128)S(1)}, s32[]{:T(128)}) while((s32[]{:T(128)}, f32[1,256,256]{2,1,0:T(8,128)S(1)}, s32[2,2]{1,0:T(2,128)S(1)}, f32[2,1,128,128]{3,2,1,0:T(8,128)S(1)}, s32[]{:T(128)}) %tuple.102), condition=%wide.while_cond.1.clone, body=%wide.while_body.1.clone.sunk | while | flops 2 | bytes 131181 | solution.py:67
  262.8 19.9 %custom-call.24 = f32[1,2,128,128]{2,3,1,0:T(8,128)S(1)} custom-call(f32[1,2,128,128]{3,2,1,0:T(8,128)S(1)} %bitcast.207), custom_call_target="InvertDiagBlocksLowerTriangular" | custom-call | tf_op jit(solution)/shard_map/vmap(jit(_solve_triangular))/triangular_solve | solution.py:67
  286.6 1.9 convolution_bitcast_fusion.1
  288.8 2.5 copy.51
  291.3 8.4 %while.15 = (s32[]{:T(128)}, f32[1,256,256]{2,1,0:T(8,128)S(1)}, s32[]{:T(128)}, f32[8,1,256,256]{3,2,1,0:T(8,128)}, s32[]{:T(128)}, /*index=5*/s32[]{:T(128)}, s32[]{:T(128)}) while((s32[]{:T(128)}, f32[1,256,256]{2,1,0:T(8,128)S(1)}, s32[]{:T(128)}, f32[8,1,256,256]{3,2,1,0:T(8,128)}, s32[]{:T(128)}, /*index=5*/s32[]{:T(128)}, ...), condition=%wide.region_5.8_spmd, body=%wide.region_4.7_spmd.sunk | while | flops 201326592 | bytes 1310835 | solution.py:51
  (114 shorter events, 36.6 us)
Async XLA Ops:
  11.3 72.7 %all-to-all-start = ((bf16[64,1,32,256]{3,2,1,0:T(8,128)(2,1)}), bf16[64,1,32,256]{3,2,1,0:T(8,128)(2,1)S(1)}, u32[]{:S(2)}, u32[]{:S(2)}) async-start(bf16[64,1,32,256]{3,2,1,0:T(8,128)(2,1)} %copy.39), calls=%async_computation | async-start | bytes 2097152 | tf_op jit(solution)/shard_map/all_to_all | solution.py:37
  30.0 60.9 %copy-start.3 = (s32[1,1,16]{2,1,0:T(1,128)S(1)}, s32[1,1,16]{2,1,0:T(1,128)}, u32[]{:S(2)}) copy-start(s32[1,1,16]{2,1,0:T(1,128)} %param.11) | copy-start | bytes 196
  30.0 61.6 %copy-start.5 = (pred[4096]{0:T(1024)(128)(4,1)S(1)}, pred[4096]{0:T(1024)(128)(4,1)}, u32[]{:S(2)}) copy-start(pred[4096]{0:T(1024)(128)(4,1)} %constant.230) | copy-start | bytes 12292
  30.0 61.6 %copy-start.6 = (pred[4096]{0:T(1024)(128)(4,1)S(1)}, pred[4096]{0:T(1024)(128)(4,1)}, u32[]{:S(2)}) copy-start(pred[4096]{0:T(1024)(128)(4,1)} %constant.231) | copy-start | bytes 12292
  30.0 61.6 %copy-start.7 = (pred[4096]{0:T(1024)(128)(4,1)S(1)}, pred[4096]{0:T(1024)(128)(4,1)}, u32[]{:S(2)}) copy-start(pred[4096]{0:T(1024)(128)(4,1)} %constant.232) | copy-start | bytes 12292
  30.1 61.6 %copy-start.8 = (pred[4096]{0:T(1024)(128)(4,1)S(1)}, pred[4096]{0:T(1024)(128)(4,1)}, u32[]{:S(2)}) copy-start(pred[4096]{0:T(1024)(128)(4,1)} %constant.233) | copy-start | bytes 12292
  30.1 61.6 %copy-start.9 = (pred[4096]{0:T(1024)(128)(4,1)S(1)}, pred[4096]{0:T(1024)(128)(4,1)}, u32[]{:S(2)}) copy-start(pred[4096]{0:T(1024)(128)(4,1)} %constant.234) | copy-start | bytes 12292
  30.1 61.6 %copy-start.10 = (pred[4096]{0:T(1024)(128)(4,1)S(1)}, pred[4096]{0:T(1024)(128)(4,1)}, u32[]{:S(2)}) copy-start(pred[4096]{0:T(1024)(128)(4,1)} %constant.235) | copy-start | bytes 12292
  30.1 61.6 %copy-start.11 = (pred[4096]{0:T(1024)(128)(4,1)S(1)}, pred[4096]{0:T(1024)(128)(4,1)}, u32[]{:S(2)}) copy-start(pred[4096]{0:T(1024)(128)(4,1)} %constant.236) | copy-start | bytes 12292
  30.1 61.6 %copy-start.12 = (pred[4096]{0:T(1024)(128)(4,1)S(1)}, pred[4096]{0:T(1024)(128)(4,1)}, u32[]{:S(2)}) copy-start(pred[4096]{0:T(1024)(128)(4,1)} %constant.237) | copy-start | bytes 12292
  30.1 61.6 %copy-start.13 = (pred[4096]{0:T(1024)(128)(4,1)S(1)}, pred[4096]{0:T(1024)(128)(4,1)}, u32[]{:S(2)}) copy-start(pred[4096]{0:T(1024)(128)(4,1)} %constant.238) | copy-start | bytes 12292
  30.1 61.6 %copy-start.14 = (pred[4096]{0:T(1024)(128)(4,1)S(1)}, pred[4096]{0:T(1024)(128)(4,1)}, u32[]{:S(2)}) copy-start(pred[4096]{0:T(1024)(128)(4,1)} %constant.239) | copy-start | bytes 12292
  30.1 61.6 %copy-start.15 = (pred[4096]{0:T(1024)(128)(4,1)S(1)}, pred[4096]{0:T(1024)(128)(4,1)}, u32[]{:S(2)}) copy-start(pred[4096]{0:T(1024)(128)(4,1)} %constant.240) | copy-start | bytes 12292
  30.2 61.6 %copy-start.16 = (pred[4096]{0:T(1024)(128)(4,1)S(1)}, pred[4096]{0:T(1024)(128)(4,1)}, u32[]{:S(2)}) copy-start(pred[4096]{0:T(1024)(128)(4,1)} %constant.241) | copy-start | bytes 12292
  30.2 61.6 %copy-start.17 = (pred[4096]{0:T(1024)(128)(4,1)S(1)}, pred[4096]{0:T(1024)(128)(4,1)}, u32[]{:S(2)}) copy-start(pred[4096]{0:T(1024)(128)(4,1)} %constant.242) | copy-start | bytes 12292
  30.2 61.6 %copy-start.18 = (pred[4096]{0:T(1024)(128)(4,1)S(1)}, pred[4096]{0:T(1024)(128)(4,1)}, u32[]{:S(2)}) copy-start(pred[4096]{0:T(1024)(128)(4,1)} %constant.243) | copy-start | bytes 12292
  30.2 61.6 %copy-start.19 = (pred[4096]{0:T(1024)(128)(4,1)S(1)}, pred[4096]{0:T(1024)(128)(4,1)}, u32[]{:S(2)}) copy-start(pred[4096]{0:T(1024)(128)(4,1)} %constant.244) | copy-start | bytes 12292
  30.2 71.9 %copy-start.20 = (s32[32]{0:T(128)S(1)}, s32[32]{0:T(128)}, u32[]{:S(2)}) copy-start(s32[32]{0:T(128)} %constant.178.clone.1) | copy-start | bytes 388
  30.2 83.0 %copy-start.4 = (s32[64,64]{1,0:T(8,128)S(1)}, s32[64,64]{1,0:T(8,128)}, u32[]{:S(2)}) copy-start(s32[64,64]{1,0:T(8,128)} %constant.179.clone.1) | copy-start | bytes 49156
  83.9 60.4 %all-to-all-start.1 = ((bf16[64,1,32,256]{3,2,1,0:T(8,128)(2,1)}), bf16[64,1,32,256]{3,2,1,0:T(8,128)(2,1)S(1)}, u32[]{:S(2)}, u32[]{:S(2)}) async-start(bf16[64,1,32,256]{3,2,1,0:T(8,128)(2,1)} %copy.40), calls=%async_computation.1 | async-start | bytes 2097152 | tf_op jit(solution)/shard_map/all_to_all | solution.py:37
  90.7 200.7 %all-gather.3.cloned.1.call-start = ((), (), s32[]{:S(2)}) async-start(), calls=%async_computation.2 | async-start | bytes 2359296 | tf_op jit(solution)/shard_map/all_gather | solution.py:43
  217.3 3.5 %copy-start = (f32[1,128,4096]{2,1,0:T(8,128)}, f32[1,128,4096]{2,1,0:T(8,128)S(1)}, u32[]{:S(2)}) copy-start(f32[1,128,4096]{2,1,0:T(8,128)S(1)} %convolution_bitcast_fusion.3) | copy-start | bytes 6291460
  282.7 1.9 copy-start.1
  291.3 8.4 %copy-start.2 = (f32[256,256]{1,0:T(8,128)S(1)}, f32[256,256]{1,0:T(8,128)}, u32[]{:S(2)}) copy-start(f32[256,256]{1,0:T(8,128)} %fusion.32) | copy-start | bytes 786436
Sparse Core Ops, SparseCore 0:
  259.1 24.0 all-gather.2
where the time goes:
time: 312 us; the launch traced here: 308 us
  other arithmetic  132 us (42%)
  waiting for transfers between devices  83.2 us (27%)
  matrix products  28.4 us (9%)
  starting transfers between devices  25.7 us (8%)
  local copies, waits for them, and re-layouts  20.3 us (7%)
  between operations  18.2 us (6%)
    all_to_all x2, waiting for transfers between devices, several_exchanges(): lax.all_to_all(share, axis, split_axis=0, concat_axis=0, tiled=True)  83.2 us
    another operation x7, other arithmetic, factor_sector(): lower_two = jnp.linalg.cholesky(gram_two)  34.8 us
    another operation x6, other arithmetic, factor_sector(): lower_one = jnp.linalg.cholesky(gram_raw + shift_value * identity)  34.4 us
    all_to_all x2, starting transfers between devices, several_exchanges(): lax.all_to_all(share, axis, split_axis=0, concat_axis=0, tiled=True)  25.4 us
    another operation x2, other arithmetic, factor_sector(): ortho_t = jax.scipy.linalg.solve_triangular(lower_two, first_t, lower=True)  19.9 us
    another operation x3, other arithmetic, factor_sector(): jax.scipy.linalg.solve_triangular(lower_one, masked.astype(jnp.float32).T...  19.7 us
    convert_element_type x2, other arithmetic, factor_sector(): gate_rows = jnp.repeat(allowed, total_rows // allowed.shape[0], total_rep...  10.3 us
    gather x1, other arithmetic, factor_sector(): jnp.repeat(allowed, total_rows // allowed.shape[0], total_repeat_length=t...  10.2 us
  transfers between devices with their start and end apart: 3, of which 2 were waited for; matrix products, arithmetic and copies ran while one was open for 18% of the time, Pallas kernels for 0%

commit v1 on v0

v1 whole, which is shorter than its diff:
```python
import jax
import jax.numpy as jnp
from jax import lax
from jax.experimental import pallas as pl
from jax.experimental.pallas import tpu as pltpu
from jax.sharding import PartitionSpec as P

B = 256
H = 128
ROWS = 64
NY, NZ = 4, 16
NB = 8
shift_value = 0.05
MESH = pl.DeviceIdType.MESH
HI = lax.Precision.HIGHEST
F32, BF16 = jnp.float32, jnp.bfloat16


def split3(x):
    a = x.astype(BF16)
    rest = x - a.astype(F32)
    b = rest.astype(BF16)
    return a, b, (rest - b.astype(F32)).astype(BF16)


def transposed_dot(x, y):
    xa, xb, xc = split3(x)
    ya, yb, yc = split3(y)
    left = jnp.concatenate([xa, xb, xa, xc, xa, xb], 0)
    right = jnp.concatenate([ya, ya, yb, ya, yc, yb], 0)
    return lax.dot_general(left, right, (((0,), (0,)), ((), ())), preferred_element_type=F32)


def dot_hi(x, y):
    return jnp.dot(x, y, precision=HI, preferred_element_type=F32)


def eliminate(w, v, base):
    row = lax.broadcasted_iota(jnp.int32, (NB, H), 0)
    cols = [jnp.broadcast_to(w[:, base + k : base + k + 1], (NB, H)) for k in range(NB)]
    pivots = jnp.zeros((NB, H), F32)
    for c in range(NB):
        p = jnp.broadcast_to(cols[c][c : c + 1, :], (NB, H))
        pivots = jnp.where(row == c, p, pivots)
        if c == NB - 1:
            break
        m = jnp.where(row > c, cols[c] * (1.0 / p), 0.0)
        for k in range(c + 1, NB):
            cols[k] = cols[k] - m * jnp.broadcast_to(cols[k][c : c + 1, :], (NB, H))
        w = w - m * jnp.broadcast_to(w[c : c + 1, :], (NB, H))
        v = v - m * jnp.broadcast_to(v[c : c + 1, :], (NB, H))
    root = lax.rsqrt(pivots)
    return w * root, v * root


def cholesky(work):
    work[:, H:] = (lax.broadcasted_iota(jnp.int32, (H, H), 0) == lax.broadcasted_iota(jnp.int32, (H, H), 1)).astype(F32)
    lane = lax.broadcasted_iota(jnp.int32, (NB, H), 1)
    row = lax.broadcasted_iota(jnp.int32, (NB, H), 0)
    for start in range(0, H, NB):
        end = start + NB
        r, v = eliminate(work[start:end, :H], work[start:end, H:], start)
        r = jnp.where(lane >= row + start, r, 0.0)
        rv = jnp.concatenate([r, v], 1)
        work[start:end, :] = rv
        if end < H:
            work[end:, :] = work[end:, :] - transposed_dot(r, rv)[end:, :]


def kernel(x, compat, sizes, q_out, acc_out, pa, pb, qa, qb, w1, w2, r_own, r_pair, pairs, c_all,
           send_sem, recv_sem, own_sem, wave_sem, out_sem, pair_send, pair_recv, ring_send, ring_recv, swap_send, swap_recv):
    b = lax.axis_index("blk")
    s = lax.axis_index("seg")
    y, z = b // NZ, lax.rem(b, NZ)
    chip, core = s // 2, lax.rem(s, 2)
    mate = chip * 2 + 1 - core
    panels = (pa, pb)

    def at(dy, dz):
        return lax.rem(y + dy, NY) * NZ + lax.rem(z + dz + NZ, NZ)

    def rows_of(k):
        return pl.ds(pl.multiple_of(k * ROWS, ROWS), ROWS)

    barrier = pltpu.get_barrier_semaphore()
    near = [{"blk": at(dy, 0)} for dy in (1, 2, 3)] + [{"blk": at(0, 1)}, {"blk": at(0, -1)}]
    near += [{"seg": mate}] + [{"seg": lax.rem(chip + d, 4) * 2 + core} for d in (1, 2, 3)]
    for to in near:
        pl.semaphore_signal(barrier, inc=1, device_id=to, device_id_type=MESH)
    pl.semaphore_wait(barrier, len(near))

    def send(half, dy, dz):
        k = at(dy, dz)
        return pltpu.make_async_remote_copy(
            src_ref=x.at[:, pl.ds(pl.multiple_of(k * B + half * H, H), H)],
            dst_ref=panels[half].at[rows_of(b), :],
            send_sem=send_sem.at[half],
            recv_sem=recv_sem.at[half, dz % NZ, dy],
            device_id={"blk": k},
            device_id_type=MESH,
        )

    def arrived(half, dy, dz):
        k = at(NY - dy, -dz)
        pltpu.make_async_remote_copy(
            src_ref=x.at[:, pl.ds(0, H)],
            dst_ref=panels[half].at[rows_of(k), :],
            send_sem=send_sem.at[half],
            recv_sem=recv_sem.at[half, dz % NZ, dy],
            device_id={"blk": k},
            device_id_type=MESH,
        ).wait_recv()

    own = [
        pltpu.make_async_copy(
            x.at[:, pl.ds(pl.multiple_of(b * B + half * H, H), H)], panels[half].at[rows_of(b), :], own_sem.at[half]
        )
        for half in (0, 1)
    ]
    own[0].start()
    own[1].start()

    def tell(direction, hop):
        pl.semaphore_signal(
            wave_sem.at[(1 - direction) // 2, hop - 1],
            inc=1,
            device_id={"blk": at(0, direction)},
            device_id_type=MESH,
        )

    tell(1, 1)
    tell(-1, 1)
    for dy in (1, 2, 3):
        send(0, dy, 0).start()
    for hop in range(1, 9):
        for direction in (1, -1):
            if hop == 8 and direction == -1:
                continue
            pl.semaphore_wait(wave_sem.at[(1 + direction) // 2, hop - 1], 1)
            if hop < 7 or (hop == 7 and direction == 1):
                tell(-direction, hop + 1)
            for dy in range(4):
                send(0, dy, direction * hop).start()
    order_b = [8] + [d * sign for d in range(7, 0, -1) for sign in (1, -1)]
    for dz in order_b:
        for dy in range(4):
            send(1, dy, dz).start()
    for dy in (1, 2, 3):
        send(1, dy, 0).start()

    n = sizes[0, 0]
    lane = lax.broadcasted_iota(jnp.int32, (H, H), 1)
    row = lax.broadcasted_iota(jnp.int32, (H, H), 0)
    live_row = [(row < n).astype(F32), (row + H < n).astype(F32)]
    live_lane = [(lane < n).astype(F32), (lane + H < n).astype(F32)]

    def collect(half, dz):
        zs = lax.rem(z - dz + NZ, NZ)
        if dz == 0:
            own[half].wait()
        for dy in range(4):
            if dy or dz:
                arrived(half, dy, dz)
        parts = []
        for ys in range(4):
            k = ys * NZ + zs
            gate = jnp.full((1, H), compat[0, ys * 4 + zs // 4], jnp.int32).astype(F32).astype(BF16)
            part = panels[half][rows_of(k), :] * gate
            panels[half][rows_of(k), :] = part
            parts.append(part)
        return jnp.concatenate(parts, 0)

    def other(dz):
        zs = lax.rem(z - dz + NZ, NZ)
        return jnp.concatenate([pa[rows_of(ys * NZ + zs), :] for ys in range(4)], 0)

    def gram(left, right):
        return lax.dot_general(left, right, (((0,), (0,)), ((), ())), preferred_element_type=F32)

    w1[:, :H] = jnp.zeros((H, H), F32)
    for dz in [0] + [d * sign for d in range(1, 8) for sign in (1, -1)] + [8]:
        part = collect(0, dz)
        w1[:, :H] += gram(part, part)
    shifted = (row == lane).astype(F32) * (shift_value * shift_value)
    w1[:, :H] = w1[:, :H] * (live_row[0] * live_lane[0] * (1.0 + shift_value)) + shifted
    cholesky(w1)
    t11 = w1[:, H:].T
    r_own[:H, :H] = w1[:, :H]
    r_own[H:, :H] = jnp.zeros((H, H), F32)

    def both(t):
        high = t.astype(BF16)
        return jnp.concatenate([high, (t - high.astype(F32)).astype(BF16)], 1)

    t1 = both(t11 * live_row[0])

    def first_columns(i, _):
        at_rows = pl.ds(pl.multiple_of(i * B, B), B)
        out = jnp.dot(pa[at_rows, :], t1, preferred_element_type=F32)
        qa[at_rows, :] = (out[:, :H] + out[:, H:]).astype(BF16)
        return 0

    lax.fori_loop(0, 16, first_columns, 0)
    write_a = pltpu.make_async_copy(qa, q_out.at[:, pl.ds(0, H)], out_sem.at[0])
    write_a.start()

    r_own[:H, H:] = jnp.zeros((H, H), F32)
    w2[:, :H] = jnp.zeros((H, H), F32)
    for dz in order_b + [0]:
        part = collect(1, dz)
        r_own[:H, H:] += gram(other(dz), part)
        w2[:, :H] += gram(part, part)
    a12 = r_own[:H, H:] * (live_row[0] * live_lane[1] * (1.0 + shift_value))
    a22 = w2[:, :H] * (live_row[1] * live_lane[1] * (1.0 + shift_value)) + shifted
    r12 = dot_hi(w1[:, H:], a12)
    r_own[:H, H:] = r12
    w2[:, :H] = a22 - transposed_dot(r12, r12)
    mixed = dot_hi(t11, r12)
    cholesky(w2)
    r_own[H:, H:] = w2[:, :H]
    to_mate = pltpu.make_async_remote_copy(
        src_ref=r_own, dst_ref=r_pair, send_sem=pair_send, recv_sem=pair_recv, device_id={"seg": mate}, device_id_type=MESH
    )
    to_mate.start()

    t22 = w2[:, H:].T
    t12 = dot_hi(mixed, t22)
    t2 = both(jnp.concatenate([-t12 * live_row[0], t22 * live_row[1]], 0))

    def last_columns(i, _):
        at_rows = pl.ds(pl.multiple_of(i * B, B), B)
        out = jnp.dot(jnp.concatenate([pa[at_rows, :], pb[at_rows, :]], 1), t2, preferred_element_type=F32)
        qb[at_rows, :] = (out[:, :H] + out[:, H:]).astype(BF16)
        return 0

    lax.fori_loop(0, 8, last_columns, 0)

    to_mate.wait()
    is_even = core == 0
    later = jnp.where(is_even, r_pair[...], r_own[...])
    earlier = jnp.where(is_even, r_own[...], r_pair[...])
    pairs[...] = dot_hi(later, earlier)
    half_rows = pl.ds(pl.multiple_of(core * H, H), H)
    ring = []
    for d in (1, 2, 3):
        copy = pltpu.make_async_remote_copy(
            src_ref=pairs.at[half_rows, :],
            dst_ref=c_all.at[chip, half_rows, :],
            send_sem=ring_send.at[d - 1],
            recv_sem=ring_recv.at[d - 1],
            device_id={"seg": lax.rem(chip + d, 4) * 2 + core},
            device_id_type=MESH,
        )
        copy.start()
        ring.append(copy)
    lax.fori_loop(8, 16, last_columns, 0)
    write_b = pltpu.make_async_copy(qb, q_out.at[:, pl.ds(H, H)], out_sem.at[1])
    write_b.start()
    swaps = []
    for d in (1, 2, 3):
        source = lax.rem(chip + 4 - d, 4)
        ring[d - 1].wait()
        copy = pltpu.make_async_remote_copy(
            src_ref=c_all.at[source, half_rows, :],
            dst_ref=c_all.at[source, half_rows, :],
            send_sem=swap_send.at[d - 1],
            recv_sem=swap_recv.at[d - 1],
            device_id={"seg": mate},
            device_id_type=MESH,
        )
        copy.start()
        swaps.append(copy)
    for copy in swaps:
        copy.wait()
    mine = jnp.where(is_even, r_own[...], pairs[...])

    @pl.when(chip == 0)
    def _():
        acc_out[...] = mine

    @pl.when(chip > 0)
    def _():
        before = lax.fori_loop(1, chip, lambda i, e: dot_hi(c_all[i], e), c_all[0])
        acc_out[...] = dot_hi(mine, before)

    for half in (0, 1):
        pltpu.make_async_remote_copy(
            src_ref=x.at[:, pl.ds(0, 63 * H)],
            dst_ref=x.at[:, pl.ds(0, 63 * H)],
            send_sem=send_sem.at[half],
            recv_sem=recv_sem.at[half, 0, 0],
            device_id={"blk": b},
            device_id_type=MESH,
        ).wait_send()
    write_a.wait()
    write_b.wait()


def local(products, compat, sizes):
    vmem, dma = pltpu.VMEM, pltpu.SemaphoreType.DMA
    ortho, acc = pl.pallas_call(
        kernel,
        out_shape=(jax.ShapeDtypeStruct((NY * NZ * ROWS, B), BF16), jax.ShapeDtypeStruct((B, B), F32)),
        in_specs=[
            pl.BlockSpec(memory_space=pl.ANY),
            pl.BlockSpec(memory_space=pltpu.SMEM),
            pl.BlockSpec(memory_space=pltpu.SMEM),
        ],
        out_specs=(pl.BlockSpec(memory_space=pl.ANY), pl.BlockSpec(memory_space=pltpu.VMEM)),
        scratch_shapes=[vmem((NY * NZ * ROWS, H), BF16)] * 4
        + [vmem((H, B), F32)] * 2
        + [vmem((B, B), F32)] * 3
        + [vmem((4, B, B), F32)]
        + [
            dma((2,)),
            dma((2, NZ, NY)),
            dma((2,)),
            pltpu.SemaphoreType.REGULAR((2, 8)),
            dma((2,)),
            dma,
            dma,
            dma((3,)),
            dma((3,)),
            dma((3,)),
            dma((3,)),
        ],
        compiler_params=pltpu.CompilerParams(collective_id=0, has_side_effects=True, vmem_limit_bytes=40 << 20),
        name="sweep",
    )(products[0], compat[0], sizes)
    return ortho[None], acc[None, None]


def solution(mesh):
    in_specs = (P("seg", "blk", None), P("seg", "blk", None), P("seg", "blk"))
    out_specs = (P("seg", None, "blk"), P("seg", "blk", None, None))
    return jax.shard_map(local, mesh=mesh, in_specs=in_specs, out_specs=out_specs, check_vma=False)
```

time: 312 us -> 135 us (0.43)
  other arithmetic: 132 us -> 0 us
  Pallas kernels: 0 us -> 127 us
  waiting for transfers between devices: 83.2 us -> 0 us
  matrix products: 28.4 us -> 0 us
  starting transfers between devices: 25.7 us -> 0 us
  between operations: 18.2 us -> 1.29 us
  local copies, waits for them, and re-layouts: 20.3 us -> 4.26 us
    pallas_call x0 -> x1, Pallas kernels: none -> 127 us  [local(): pl.pallas_call(kernel, out_shape=(jax.ShapeDtypeStruct((NY * NZ * ROWS, B...]
    another operation x18 -> x0, other arithmetic: 109 us -> none  [the longest x7 34.8 us: factor_sector(): lower_two = jnp.linalg.cholesky(gram_two)]
    all_to_all x2 -> x0, waiting for transfers between devices: 83.2 us -> none  [several_exchanges(): lax.all_to_all(share, axis, split_axis=0, concat_axis=0, tiled=True)]
    all_to_all x2 -> x0, starting transfers between devices: 25.4 us -> none  [several_exchanges(): lax.all_to_all(share, axis, split_axis=0, concat_axis=0, tiled=True)]
    dot_general x10 -> x0, matrix products: 15.9 us -> none  [the longest x7 9.12 us: compose(): jnp.einsum('kab,kbc->kac', later, earlier, precision=lax.Precision.HIGHEST)]
    another operation x10 -> x0, matrix products: 12.5 us -> none  [the longest x3 5.79 us: factor_sector(): jax.scipy.linalg.solve_triangular(lower_one, masked.astype(jnp.float32).T...]
    another operation x22 -> x0, local copies, waits for them, and re-layouts: 10.9 us -> none  [the longest x9 4.04 us: factor_sector(): jax.scipy.linalg.solve_triangular(lower_one, masked.astype(jnp.float32).T...]
    convert_element_type x5 -> x0, other arithmetic: 10.6 us -> none  [the longest x2 10.3 us: factor_sector(): gate_rows = jnp.repeat(allowed, total_rows // allowed.shape[0], total_rep...]
  transfers between devices with their start and end apart: 3 -> 0, of which waited for: 2 -> 0; matrix products, arithmetic and copies ran while one was open for 18% -> 0% of each run, Pallas kernels for 0% -> 0%
where the time goes in v1:
time: 135 us; the launch traced here: 132 us
  Pallas kernels  127 us (94%)
  local copies, waits for them, and re-layouts  4.26 us (3%)
    pallas_call x1, Pallas kernels, local(): pl.pallas_call(kernel, out_shape=(jax.ShapeDtypeStruct((NY * NZ * ROWS, B...  127 us
    unnamed x6, local copies, waits for them, and re-layouts  4.26 us

profile of v1, /device:TPU:6, one launch (start us, length us, event | category | flops | bytes accessed | tf_op | source)
XLA Modules:
  0.0 132.3 jit_solution(16125662718524621812)
XLA Ops:
  1.3 0.0 copy-start
  1.3 1.6 %copy-done = bf16[1,64,16384]{2,1,0:T(8,128)(2,1)S(1)} copy-done((bf16[1,64,16384]{2,1,0:T(8,128)(2,1)S(1)}, bf16[1,64,16384]{2,1,0:T(8,128)(2,1)}, u32[]{:S(2)}) %copy-start) | copy-done | bytes 2097176
  2.9 0.0 copy-start.1
  2.9 0.7 copy-done.1
  3.5 126.8 %sweep.1 = (bf16[4096,256]{1,0:T(8,128)(2,1)S(1)}, f32[256,256]{1,0:T(8,128)S(1)}) custom-call(bf16[64,16384]{1,0:T(8,128)(2,1)S(1)} %bitcast.4, s32[1,16]{1,0:T(1,128)S(1)} %bitcast.7, s32[1,1]{1,0:T(1,128)S(6)} %copy.7.sizes), custom_call_target="tpu_custom_call" | custom-call | tf_op jit(solution)/shard_map/sweep/pallas_call | solution.py:301
  130.3 1.3 copy.8
  131.6 0.7 copy.9
Async XLA Ops:
  1.3 1.6 %copy-start = (bf16[1,64,16384]{2,1,0:T(8,128)(2,1)S(1)}, bf16[1,64,16384]{2,1,0:T(8,128)(2,1)}, u32[]{:S(2)}) copy-start(bf16[1,64,16384]{2,1,0:T(8,128)(2,1)} %param.3) | copy-start | bytes 6291460
  2.9 0.7 copy-start.1

commit v2 on v1

--- a/solution.py
+++ b/solution.py
@@ -10,6 +10,7 @@
 ROWS = 64
 NY, NZ = 4, 16
 NB = 8
+SUPER = 32
 shift_value = 0.05
 MESH = pl.DeviceIdType.MESH
 HI = lax.Precision.HIGHEST
@@ -35,40 +36,57 @@
     return jnp.dot(x, y, precision=HI, preferred_element_type=F32)
 
 
+def spread(x, r):
+    return jnp.broadcast_to(x[r : r + 1, :], (NB, H))
+
+
 def eliminate(w, v, base):
+    groups = len(w)
     row = lax.broadcasted_iota(jnp.int32, (NB, H), 0)
-    cols = [jnp.broadcast_to(w[:, base + k : base + k + 1], (NB, H)) for k in range(NB)]
-    pivots = jnp.zeros((NB, H), F32)
-    for c in range(NB):
-        p = jnp.broadcast_to(cols[c][c : c + 1, :], (NB, H))
-        pivots = jnp.where(row == c, p, pivots)
-        if c == NB - 1:
-            break
-        m = jnp.where(row > c, cols[c] * (1.0 / p), 0.0)
-        for k in range(c + 1, NB):
-            cols[k] = cols[k] - m * jnp.broadcast_to(cols[k][c : c + 1, :], (NB, H))
-        w = w - m * jnp.broadcast_to(w[c : c + 1, :], (NB, H))
-        v = v - m * jnp.broadcast_to(v[c : c + 1, :], (NB, H))
-    root = lax.rsqrt(pivots)
-    return w * root, v * root
+    for g in range(groups):
+        first = base + NB * g
+        cols = [[jnp.broadcast_to(w[h][:, first + k : first + k + 1], (NB, H)) for k in range(NB)] for h in range(g, groups)]
+        pivots = jnp.zeros((NB, H), F32)
+        for c in range(NB):
+            p = spread(cols[0][c], c)
+            pivots = jnp.where(row == c, p, pivots)
+            if c == NB - 1 and g == groups - 1:
+                break
+            q = 1.0 / p
+            m = [cols[h - g][c] * q for h in range(g, groups)]
+            m[0] = jnp.where(row > c, m[0], 0.0)
+            for k in range(c + 1, NB):
+                along = spread(cols[0][k], c)
+                for h in range(g, groups):
+                    cols[h - g][k] = cols[h - g][k] - m[h - g] * along
+            w_row, v_row = spread(w[g], c), spread(v[g], c)
+            for h in range(g + (c == NB - 1), groups):
+                w[h] = w[h] - m[h - g] * w_row
+                v[h] = v[h] - m[h - g] * v_row
+        root = lax.rsqrt(pivots)
+        w[g] = w[g] * root
+        v[g] = v[g] * root
+    return w, v
 
 
 def cholesky(work):
     work[:, H:] = (lax.broadcasted_iota(jnp.int32, (H, H), 0) == lax.broadcasted_iota(jnp.int32, (H, H), 1)).astype(F32)
-    lane = lax.broadcasted_iota(jnp.int32, (NB, H), 1)
-    row = lax.broadcasted_iota(jnp.int32, (NB, H), 0)
-    for start in range(0, H, NB):
-        end = start + NB
-        r, v = eliminate(work[start:end, :H], work[start:end, H:], start)
-        r = jnp.where(lane >= row + start, r, 0.0)
-        rv = jnp.concatenate([r, v], 1)
+    lane = lax.broadcasted_iota(jnp.int32, (SUPER, H), 1)
+    row = lax.broadcasted_iota(jnp.int32, (SUPER, H), 0)
+    for start in range(0, H, SUPER):
+        end = start + SUPER
+        pieces = range(start, end, NB)
+        w, v = eliminate([work[i : i + NB, :H] for i in pieces], [work[i : i + NB, H:] for i in pieces], start)
+        r = jnp.where(lane >= row + start, jnp.concatenate(w, 0), 0.0)
+        rv = jnp.concatenate([r, jnp.concatenate(v, 0)], 1)
         work[start:end, :] = rv
         if end < H:
             work[end:, :] = work[end:, :] - transposed_dot(r, rv)[end:, :]
 
 
-def kernel(x, compat, sizes, q_out, acc_out, pa, pb, qa, qb, w1, w2, r_own, r_pair, pairs, c_all,
-           send_sem, recv_sem, own_sem, wave_sem, out_sem, pair_send, pair_recv, ring_send, ring_recv, swap_send, swap_recv):
+def kernel(x, compat_in, sizes_in, q_out, acc_out, pa, pb, qa, qb, w1, w2, c_all, pairs, run,
+           send_sem, recv_sem, own_sem, wave_sem, out_sem, mate_send, mate_recv, ring_send, ring_recv, swap_send, swap_recv,
+           compat, sizes, table_sem):
     b = lax.axis_index("blk")
     s = lax.axis_index("seg")
     y, z = b // NZ, lax.rem(b, NZ)
@@ -81,6 +99,13 @@
 
     def rows_of(k):
         return pl.ds(pl.multiple_of(k * ROWS, ROWS), ROWS)
+
+    tables = [
+        pltpu.make_async_copy(compat_in, compat, table_sem.at[0]),
+        pltpu.make_async_copy(sizes_in, sizes, table_sem.at[1]),
+    ]
+    for copy in tables:
+        copy.start()
 
     barrier = pltpu.get_barrier_semaphore()
     near = [{"blk": at(dy, 0)} for dy in (1, 2, 3)] + [{"blk": at(0, 1)}, {"blk": at(0, -1)}]
@@ -148,6 +173,8 @@
     for dy in (1, 2, 3):
         send(1, dy, 0).start()
 
+    for copy in tables:
+        copy.wait()
     n = sizes[0, 0]
     lane = lax.broadcasted_iota(jnp.int32, (H, H), 1)
     row = lax.broadcasted_iota(jnp.int32, (H, H), 0)
@@ -177,6 +204,61 @@
     def gram(left, right):
         return lax.dot_general(left, right, (((0,), (0,)), ((), ())), preferred_element_type=F32)
 
+    places = ((0, 0), (0, H), (H, H))
+
+    def block(site, part):
+        at_row, at_lane = places[part]
+        return c_all.at[site, pl.ds(at_row, H), pl.ds(at_lane, H)]
+
+    def over_chip(part):
+        return pltpu.make_async_remote_copy(
+            src_ref=block(s, part),
+            dst_ref=block(s, part),
+            send_sem=mate_send.at[part],
+            recv_sem=mate_recv.at[part],
+            device_id={"seg": mate},
+            device_id_type=MESH,
+        )
+
+    def over_ring(part, d):
+        return pltpu.make_async_remote_copy(
+            src_ref=block(s, part),
+            dst_ref=block(s, part),
+            send_sem=ring_send.at[part, d - 1],
+            recv_sem=ring_recv.at[part, d - 1],
+            device_id={"seg": lax.rem(chip + d, 4) * 2 + core},
+            device_id_type=MESH,
+        )
+
+    def hand_on(part, d):
+        site = lax.rem(chip + 4 - d, 4) * 2 + core
+        return pltpu.make_async_remote_copy(
+            src_ref=block(site, part),
+            dst_ref=block(site, part),
+            send_sem=swap_send.at[part, d - 1],
+            recv_sem=swap_recv.at[part, d - 1],
+            device_id={"seg": mate},
+            device_id_type=MESH,
+        )
+
+    def give(part):
+        for d in (1, 3, 2):
+            over_ring(part, d).start()
+        over_chip(part).start()
+
+    def relay(part):
+        for d in (1, 3, 2):
+            over_ring(part, d).wait()
+            hand_on(part, d).start()
+
+    def settle(part):
+        over_chip(part).wait()
+        for d in (1, 3, 2):
+            hand_on(part, d).wait()
+
+    for site in range(8):
+        c_all[site, H:, :H] = jnp.zeros((H, H), F32)
+
     w1[:, :H] = jnp.zeros((H, H), F32)
     for dz in [0] + [d * sign for d in range(1, 8) for sign in (1, -1)] + [8]:
         part = collect(0, dz)
@@ -184,9 +266,8 @@
     shifted = (row == lane).astype(F32) * (shift_value * shift_value)
     w1[:, :H] = w1[:, :H] * (live_row[0] * live_lane[0] * (1.0 + shift_value)) + shifted
     cholesky(w1)
+    c_all[s, :H, :H] = w1[:, :H]
     t11 = w1[:, H:].T
-    r_own[:H, :H] = w1[:, :H]
-    r_own[H:, :H] = jnp.zeros((H, H), F32)
 
     def both(t):
         high = t.astype(BF16)
@@ -201,31 +282,66 @@
         return 0
 
     lax.fori_loop(0, 16, first_columns, 0)
+    give(0)
     write_a = pltpu.make_async_copy(qa, q_out.at[:, pl.ds(0, H)], out_sem.at[0])
     write_a.start()
 
-    r_own[:H, H:] = jnp.zeros((H, H), F32)
+    def collect_last(groups):
+        for dz in groups:
+            part = collect(1, dz)
+            c_all[s, :H, H:] += gram(other(dz), part)
+            w2[:, :H] += gram(part, part)
+
+    c_all[s, :H, H:] = jnp.zeros((H, H), F32)
     w2[:, :H] = jnp.zeros((H, H), F32)
-    for dz in order_b + [0]:
-        part = collect(1, dz)
-        r_own[:H, H:] += gram(other(dz), part)
-        w2[:, :H] += gram(part, part)
-    a12 = r_own[:H, H:] * (live_row[0] * live_lane[1] * (1.0 + shift_value))
+    collect_last(order_b[:9])
+    relay(0)
+    settle(0)
+    for i in range(4):
+        pairs[i, H:, :H] = jnp.zeros((H, H), F32)
+        pairs[i, :H, :H] = dot_hi(c_all[2 * i + 1, :H, :H], c_all[2 * i, :H, :H])
+    is_even = core == 0
+
+    upper, right, whole = slice(0, H), slice(H, B), slice(0, B)
+    acc_out[H:, :H] = jnp.zeros((H, H), F32)
+
+    def last_product(rows, lanes):
+        mine = jnp.where(is_even, c_all[s, rows, rows], pairs[chip, rows, rows])
+
+        @pl.when(chip == 0)
+        def _():
+            acc_out[rows, lanes] = jnp.where(is_even, c_all[s, rows, lanes], pairs[chip, rows, lanes])
+
+        @pl.when(chip > 0)
+        def _():
+            run[rows, :] = pairs[0, rows, lanes]
+
+        for i in (1, 2):
+
+            @pl.when(chip > i)
+            def _():
+                run[rows, :] = dot_hi(pairs[i, rows, rows], run[rows, :])
+
+        @pl.when(chip > 0)
+        def _():
+            acc_out[rows, lanes] = dot_hi(mine, run[rows, :])
+
+    last_product(upper, upper)
+    collect_last(order_b[9:] + [0])
+    a12 = c_all[s, :H, H:] * (live_row[0] * live_lane[1] * (1.0 + shift_value))
     a22 = w2[:, :H] * (live_row[1] * live_lane[1] * (1.0 + shift_value)) + shifted
     r12 = dot_hi(w1[:, H:], a12)
-    r_own[:H, H:] = r12
+    c_all[s, :H, H:] = r12
     w2[:, :H] = a22 - transposed_dot(r12, r12)
     mixed = dot_hi(t11, r12)
+    give(1)
     cholesky(w2)
-    r_own[H:, H:] = w2[:, :H]
-    to_mate = pltpu.make_async_remote_copy(
-        src_ref=r_own, dst_ref=r_pair, send_sem=pair_send, recv_sem=pair_recv, device_id={"seg": mate}, device_id_type=MESH
-    )
-    to_mate.start()
-
+    c_all[s, H:, H:] = w2[:, :H]
     t22 = w2[:, H:].T
     t12 = dot_hi(mixed, t22)
     t2 = both(jnp.concatenate([-t12 * live_row[0], t22 * live_row[1]], 0))
+    give(2)
+    relay(1)
 
     def last_columns(i, _):
         at_rows = pl.ds(pl.multiple_of(i * B, B), B)
@@ -233,55 +349,15 @@
         qb[at_rows, :] = (out[:, :H] + out[:, H:]).astype(BF16)
         return 0
 
-    lax.fori_loop(0, 8, last_columns, 0)
-
-    to_mate.wait()
-    is_even = core == 0
-    later = jnp.where(is_even, r_pair[...], r_own[...])
-    earlier = jnp.where(is_even, r_own[...], r_pair[...])
-    pairs[...] = dot_hi(later, earlier)
-    half_rows = pl.ds(pl.multiple_of(core * H, H), H)
-    ring = []
-    for d in (1, 2, 3):
-        copy = pltpu.make_async_remote_copy(
-            src_ref=pairs.at[half_rows, :],
-            dst_ref=c_all.at[chip, half_rows, :],
-            send_sem=ring_send.at[d - 1],
-            recv_sem=ring_recv.at[d - 1],
-            device_id={"seg": lax.rem(chip + d, 4) * 2 + core},
-            device_id_type=MESH,
-        )
-        copy.start()
-        ring.append(copy)
-    lax.fori_loop(8, 16, last_columns, 0)
+    lax.fori_loop(0, 16, last_columns, 0)
     write_b = pltpu.make_async_copy(qb, q_out.at[:, pl.ds(H, H)], out_sem.at[1])
     write_b.start()
-    swaps = []
-    for d in (1, 2, 3):
-        source = lax.rem(chip + 4 - d, 4)
-        ring[d - 1].wait()
-        copy = pltpu.make_async_remote_copy(
-            src_ref=c_all.at[source, half_rows, :],
-            dst_ref=c_all.at[source, half_rows, :],
-            send_sem=swap_send.at[d - 1],
-            recv_sem=swap_recv.at[d - 1],
-            device_id={"seg": mate},
-            device_id_type=MESH,
-        )
-        copy.start()
-        swaps.append(copy)
-    for copy in swaps:
-        copy.wait()
-    mine = jnp.where(is_even, r_own[...], pairs[...])
-
-    @pl.when(chip == 0)
-    def _():
-        acc_out[...] = mine
-
-    @pl.when(chip > 0)
-    def _():
-        before = lax.fori_loop(1, chip, lambda i, e: dot_hi(c_all[i], e), c_all[0])
-        acc_out[...] = dot_hi(mine, before)
+    settle(1)
+    relay(2)
+    settle(2)
+    for i in range(4):
+        pairs[i, :, H:] = dot_hi(c_all[2 * i + 1], c_all[2 * i, :, H:])
+    last_product(whole, right)
 
     for half in (0, 1):
         pltpu.make_async_remote_copy(
@@ -302,27 +378,29 @@
         kernel,
         out_shape=(jax.ShapeDtypeStruct((NY * NZ * ROWS, B), BF16), jax.ShapeDtypeStruct((B, B), F32)),
         in_specs=[
-            pl.BlockSpec(memory_space=pl.ANY),
-            pl.BlockSpec(memory_space=pltpu.SMEM),
-            pl.BlockSpec(memory_space=pltpu.SMEM),
+            pl.BlockSpec(memory_space=pltpu.HBM),
+            pl.BlockSpec(memory_space=pltpu.HBM),
+            pl.BlockSpec(memory_space=pltpu.HBM),
         ],
         out_specs=(pl.BlockSpec(memory_space=pl.ANY), pl.BlockSpec(memory_space=pltpu.VMEM)),
         scratch_shapes=[vmem((NY * NZ * ROWS, H), BF16)] * 4
         + [vmem((H, B), F32)] * 2
-        + [vmem((B, B), F32)] * 3
-        + [vmem((4, B, B), F32)]
+        + [vmem((8, B, B), F32), vmem((4, B, B), F32), vmem((B, H), F32)]
         + [
             dma((2,)),
             dma((2, NZ, NY)),
             dma((2,)),
             pltpu.SemaphoreType.REGULAR((2, 8)),
             dma((2,)),
-            dma,
-            dma,
             dma((3,)),
             dma((3,)),
-            dma((3,)),
-            dma((3,)),
+            dma((3, 3)),
+            dma((3, 3)),
+            dma((3, 3)),
+            dma((3, 3)),
+            pltpu.SMEM((1, 16), jnp.int32),
+            pltpu.SMEM((1, 1), jnp.int32),
+            dma((2,)),
         ],
         compiler_params=pltpu.CompilerParams(collective_id=0, has_side_effects=True, vmem_limit_bytes=40 << 20),
         name="sweep",

time: 135 us -> 128 us (0.948)
  Pallas kernels: 127 us -> 120 us
    pallas_call x1, Pallas kernels: 127 us -> 120 us  [local(): pl.pallas_call(kernel, out_shape=(jax.ShapeDtypeStruct((NY * NZ * ROWS, B...]
where the time goes in v2:
time: 128 us; the launch traced here: 126 us
  Pallas kernels  120 us (94%)
  local copies, waits for them, and re-layouts  4.26 us (3%)
  between operations  1.29 us (1%)
    pallas_call x1, Pallas kernels, local(): pl.pallas_call(kernel, out_shape=(jax.ShapeDtypeStruct((NY * NZ * ROWS, B...  120 us
    unnamed x6, local copies, waits for them, and re-layouts  4.26 us

profile of v2, /device:TPU:6, one launch (start us, length us, event | category | flops | bytes accessed | tf_op | source)
XLA Modules:
  0.0 125.8 jit_solution(3534839248251896359)
XLA Ops:
  1.3 0.0 copy-start
  1.3 1.6 %copy-done = bf16[1,64,16384]{2,1,0:T(8,128)(2,1)S(1)} copy-done((bf16[1,64,16384]{2,1,0:T(8,128)(2,1)S(1)}, bf16[1,64,16384]{2,1,0:T(8,128)(2,1)}, u32[]{:S(2)}) %copy-start) | copy-done | bytes 2097176
  2.9 0.0 copy-start.1
  2.9 0.7 copy-done.1
  3.5 120.2 %sweep.1 = (bf16[4096,256]{1,0:T(8,128)(2,1)S(1)}, f32[256,256]{1,0:T(8,128)S(1)}) custom-call(bf16[64,16384]{1,0:T(8,128)(2,1)S(1)} %bitcast.4, s32[1,16]{1,0:T(1,128)S(1)} %bitcast.7, s32[1,1]{1,0:T(1,128)S(6)} %copy.7.sizes_in), custom_call_target="tpu_custom_call" | custom-call | tf_op jit(solution)/shard_map/sweep/pallas_call | solution.py:377
  123.7 1.3 %copy.8 = bf16[1,4096,256]{2,1,0:T(8,128)(2,1)} copy(bf16[1,4096,256]{2,1,0:T(8,128)(2,1)S(1)} %bitcast.5) | data formatting | bytes 4194304
  125.1 0.7 copy.9
Async XLA Ops:
  1.3 1.6 %copy-start = (bf16[1,64,16384]{2,1,0:T(8,128)(2,1)S(1)}, bf16[1,64,16384]{2,1,0:T(8,128)(2,1)}, u32[]{:S(2)}) copy-start(bf16[1,64,16384]{2,1,0:T(8,128)(2,1)} %param.3) | copy-start | bytes 6291460
  2.9 0.7 copy-start.1

commit v3 on v2

--- a/solution.py
+++ b/solution.py
@@ -34,6 +34,13 @@
 
 def dot_hi(x, y):
     return jnp.dot(x, y, precision=HI, preferred_element_type=F32)
+
+
+def product(x, y):
+    xh, yh = x.astype(BF16), y.astype(BF16)
+    xl, yl = (x - xh.astype(F32)).astype(BF16), (y - yh.astype(F32)).astype(BF16)
+    left, right = jnp.concatenate([xh, xh, xl], 1), jnp.concatenate([yh, yl, yh], 0)
+    return jnp.dot(left, right, preferred_element_type=F32)
 
 
 def spread(x, r):
@@ -299,7 +306,7 @@
     settle(0)
     for i in range(4):
         pairs[i, H:, :H] = jnp.zeros((H, H), F32)
-        pairs[i, :H, :H] = dot_hi(c_all[2 * i + 1, :H, :H], c_all[2 * i, :H, :H])
+        pairs[i, :H, :H] = product(c_all[2 * i + 1, :H, :H], c_all[2 * i, :H, :H])
     is_even = core == 0
 
     upper, right, whole = slice(0, H), slice(H, B), slice(0, B)
@@ -320,11 +327,11 @@
 
             @pl.when(chip > i)
             def _():
-                run[rows, :] = dot_hi(pairs[i, rows, rows], run[rows, :])
+                run[rows, :] = product(pairs[i, rows, rows], run[rows, :])
 
         @pl.when(chip > 0)
         def _():
-            acc_out[rows, lanes] = dot_hi(mine, run[rows, :])
+            acc_out[rows, lanes] = product(mine, run[rows, :])
 
     last_product(upper, upper)
     collect_last(order_b[9:] + [0])
@@ -341,7 +348,6 @@
     t12 = dot_hi(mixed, t22)
     t2 = both(jnp.concatenate([-t12 * live_row[0], t22 * live_row[1]], 0))
     give(2)
-    relay(1)
 
     def last_columns(i, _):
         at_rows = pl.ds(pl.multiple_of(i * B, B), B)
@@ -352,11 +358,16 @@
     lax.fori_loop(0, 16, last_columns, 0)
     write_b = pltpu.make_async_copy(qb, q_out.at[:, pl.ds(H, H)], out_sem.at[1])
     write_b.start()
+    relay(1)
     settle(1)
+    for i in range(4):
+        pairs[i, :H, H:] = product(c_all[2 * i + 1, :H, :H], c_all[2 * i, :H, H:])
     relay(2)
     settle(2)
     for i in range(4):
-        pairs[i, :, H:] = dot_hi(c_all[2 * i + 1], c_all[2 * i, :, H:])
+        late = product(c_all[2 * i + 1, :, H:], c_all[2 * i, H:, H:])
+        pairs[i, :H, H:] += late[:H]
+        pairs[i, H:, H:] = late[H:]
     last_product(whole, right)
 
     for half in (0, 1):

time: 128 us -> 127 us (level)
  no operation moved by 1% of the time
where the time goes in v3:
time: 127 us; the launch traced here: 125 us
  Pallas kernels  120 us (94%)
  local copies, waits for them, and re-layouts  4.26 us (3%)
  between operations  1.29 us (1%)
    pallas_call x1, Pallas kernels, local(): pl.pallas_call(kernel, out_shape=(jax.ShapeDtypeStruct((NY * NZ * ROWS, B...  120 us
    unnamed x6, local copies, waits for them, and re-layouts  4.26 us

profile of v3, /device:TPU:6, one launch (start us, length us, event | category | flops | bytes accessed | tf_op | source)
XLA Modules:
  0.0 125.5 jit_solution(6799591974316365465)
XLA Ops:
  1.3 0.0 copy-start
  1.3 1.6 %copy-done = bf16[1,64,16384]{2,1,0:T(8,128)(2,1)S(1)} copy-done((bf16[1,64,16384]{2,1,0:T(8,128)(2,1)S(1)}, bf16[1,64,16384]{2,1,0:T(8,128)(2,1)}, u32[]{:S(2)}) %copy-start) | copy-done | bytes 2097176
  2.9 0.0 copy-start.1
  2.9 0.7 copy-done.1
  3.5 119.9 %sweep.1 = (bf16[4096,256]{1,0:T(8,128)(2,1)S(1)}, f32[256,256]{1,0:T(8,128)S(1)}) custom-call(bf16[64,16384]{1,0:T(8,128)(2,1)S(1)} %bitcast.4, s32[1,16]{1,0:T(1,128)S(1)} %bitcast.7, s32[1,1]{1,0:T(1,128)S(6)} %copy.7.sizes_in), custom_call_target="tpu_custom_call" | custom-call | tf_op jit(solution)/shard_map/sweep/pallas_call | solution.py:388
  123.5 1.3 %copy.8 = bf16[1,4096,256]{2,1,0:T(8,128)(2,1)} copy(bf16[1,4096,256]{2,1,0:T(8,128)(2,1)S(1)} %bitcast.5) | data formatting | bytes 4194304
  124.8 0.7 copy.9
Async XLA Ops:
  1.3 1.6 %copy-start = (bf16[1,64,16384]{2,1,0:T(8,128)(2,1)S(1)}, bf16[1,64,16384]{2,1,0:T(8,128)(2,1)}, u32[]{:S(2)}) copy-start(bf16[1,64,16384]{2,1,0:T(8,128)(2,1)} %param.3) | copy-start | bytes 6291460
  2.9 0.7 copy-start.1
